TPU v7x, 256 devices: a whole 4x4x8 slice. The times are simulated.
256 devices in a mesh: group: 16 (over z, core), shard: 16 (over y, x).
Axes of the slice: x: 4, y: 4, z: 8, core: 2. Of those that a mesh axis runs over, the one named last changes fastest.
Arguments:
- tokens: bfloat16 [512, 1280], P(('group', 'shard')), as said below
- kv_cache: bfloat16 [512, 128, 2560], P(('group', 'shard'))
- keep_list: int32 [512, 128], P(('group', 'shard')), may hold values from 0 to 1
- lengths: int32 [512], P(('group', 'shard')), may hold values from 64 to 128
- merge_index: int32 [512, 128], P(('group', 'shard')), may hold values from 0 to 15
- merge_table: bfloat16 [16], replicated, may hold values from 0.0099487305 to 0.099609375
- move_offset: int32 [16, 2], P('shard'), may hold values from 0 to 15, as said below
- pair_mask: int32 [16], P('shard'), may hold values from 1 to 15
- w_qkv: bfloat16 [1280, 3840], P(None, 'shard'), may hold values from -0.15625 to 0.15625
- w_out: bfloat16 [1280, 1280], P(None, 'shard'), may hold values from -0.15625 to 0.15625
- w_up: bfloat16 [1280, 5120], P(None, 'shard'), may hold values from -0.15625 to 0.15625
- w_gate: bfloat16 [1280, 5120], P(None, 'shard'), may hold values from -0.15625 to 0.15625
- w_down: bfloat16 [5120, 1280], P('shard'), may hold values from -0.078125 to 0.078125
- qk_scale: float32 [1280], replicated, may hold values from 0.5 to 2
- attn_rate: float32 [1280], replicated, may hold values from 0.05 to 0.5
- mlp_rate: float32 [1280], replicated, may hold values from 0.05 to 0.5
- up_scale: float32 [5120], P('shard'), may hold values from 0.5 to 2
- gate_scale: float32 [5120], P('shard'), may hold values from 0.5 to 2
Outputs:
- new_hidden: bfloat16 [512, 1280], P(('group', 'shard'))
- moved_cache: bfloat16 [512, 128, 2560], P(('group', 'shard'))
Inputs may be any that keep to these rules, and one draw needn't show every extreme that they name: `tokens`: slot 1 of group g and shard s holds the same token as that slot of group g XOR pair_mask[s] on shard s. `move_offset`: the 2 offsets of one shard index are distinct.
All inputs are finite; a program needn't handle non-finite values.
Results may differ from a plain program's by a relative error of at most 0.011.
Values may be sent and summed in bfloat16 or wider, within the bound.
A program may use at most 128 MiB of HBM per device.

v0:
```python
import jax
import jax.numpy as jnp
from jax import lax
from jax.sharding import PartitionSpec as P

DH = 64
BLOCK = 128
WTAB = 16
EPSILON = 1e-06
NEGATIVE = -1e30


def rms_normal(vector):
    return vector * lax.rsqrt(jnp.mean(vector * vector, axis=-1, keepdims=True) + EPSILON)


def head_normal(vector, scaling):
    return vector * lax.rsqrt(jnp.sum(vector * vector, axis=-1, keepdims=True) + EPSILON) * scaling


def rounded(vector):
    return lax.optimization_barrier(vector.astype(jnp.bfloat16)).astype(jnp.float32)


def spread_columns(row_block, weight):
    columns = jnp.dot(
        lax.all_gather(row_block, "shard", axis=0, tiled=True),
        weight,
        preferred_element_type=jnp.float32,
    ).astype(jnp.bfloat16)
    return lax.all_to_all(columns, "shard", split_axis=0, concat_axis=1, tiled=True)


def compact_local(kv_cache, keep_list, lengths, merge_index, merge_table):
    slot_count, context, doubled = kv_cache.shape
    block_count = context // BLOCK
    in_length = jnp.arange(context, dtype=jnp.int32)[None, :] < lengths[:, None]
    keeper = (keep_list == 1) & in_length
    dropper = (keep_list == 0) & in_length
    position = jnp.cumsum(keeper.astype(jnp.int32), axis=1) - 1
    kept_count = jnp.sum(keeper.astype(jnp.int32), axis=1)
    drop_count = jnp.sum(dropper.astype(jnp.int32), axis=1)
    table_hits = merge_index[:, :, None] == jnp.arange(WTAB, dtype=jnp.int32)[None, None, :]
    weights = jnp.sum(
        jnp.where(table_hits, merge_table.astype(jnp.float32)[None, None, :], 0.0), axis=2
    ) * dropper.astype(jnp.float32)
    target = jnp.arange(BLOCK, dtype=jnp.int32)
    placing = (position[:, None, :] == target[None, :, None]) & keeper[:, None, :]
    summing = jnp.where(
        target[None, :, None] == kept_count[:, None, None], weights[:, None, :], 0.0
    )
    mixing = (placing.astype(jnp.float32) + summing).astype(jnp.bfloat16)
    packed = jnp.einsum(
        "ndk,nkc->ndc", mixing, kv_cache, preferred_element_type=jnp.float32
    ).astype(jnp.bfloat16)
    live_count = (kept_count + (drop_count > 0).astype(jnp.int32)).reshape(slot_count, block_count)
    return (packed, live_count.astype(jnp.bfloat16))


def per_device(
    tokens,
    kv_cache,
    keep_list,
    lengths,
    merge_index,
    merge_table,
    move_offset,
    pair_mask,
    w_qkv,
    w_out,
    w_up,
    w_gate,
    w_down,
    qk_scale,
    attn_rate,
    mlp_rate,
    up_scale,
    gate_scale,
):
    slot_count, context, doubled = kv_cache.shape
    model_width = tokens.shape[1]
    head_count = model_width // DH
    group_count = lax.axis_size("group")
    group_index = lax.axis_index("group")
    packed, live_count = compact_local(kv_cache, keep_list, lengths, merge_index, merge_table)
    offsets = move_offset[0]
    target = (group_index + offsets) % group_count
    sender = (jnp.arange(group_count, dtype=jnp.int32)[:, None] == target[None, :]).astype(
        jnp.bfloat16
    )
    outgoing = jnp.einsum("pj,jrc->prc", sender, packed, preferred_element_type=jnp.float32).astype(
        jnp.bfloat16
    )
    outgoing_live = jnp.einsum(
        "pj,jb->pb", sender, live_count, preferred_element_type=jnp.float32
    ).astype(jnp.bfloat16)
    incoming, incoming_live = (
        lax.all_to_all(outgoing, "group", split_axis=0, concat_axis=0, tiled=True),
        lax.all_to_all(outgoing_live, "group", split_axis=0, concat_axis=0, tiled=True),
    )
    source = (group_index - offsets) % group_count
    picker = (source[:, None] == jnp.arange(group_count, dtype=jnp.int32)[None, :]).astype(
        jnp.bfloat16
    )
    moved_cache = jnp.einsum(
        "jp,prc->jrc", picker, incoming, preferred_element_type=jnp.float32
    ).astype(jnp.bfloat16)
    moved_live = jnp.einsum("jp,pb->jb", picker, incoming_live, preferred_element_type=jnp.float32)
    projected = spread_columns(tokens, w_qkv)
    head_scale = qk_scale.reshape(head_count, DH)
    queries = head_normal(
        projected[:, :model_width].astype(jnp.float32).reshape(slot_count, head_count, DH),
        head_scale,
    ).astype(jnp.bfloat16)
    new_keys = head_normal(
        projected[:, model_width : 2 * model_width]
        .astype(jnp.float32)
        .reshape(slot_count, head_count, DH),
        head_scale,
    ).astype(jnp.bfloat16)
    new_values = projected[:, 2 * model_width :].reshape(slot_count, head_count, DH)
    key_rows = moved_cache[:, :, :model_width].reshape(slot_count, context, head_count, DH)
    value_rows = moved_cache[:, :, model_width:].reshape(slot_count, context, head_count, DH)
    score_scale = float(DH) ** 0.5
    scores = score_scale * jnp.einsum(
        "jhd,jrhd->jhr", queries, key_rows, preferred_element_type=jnp.float32
    )
    fresh_score = score_scale * jnp.sum(
        queries.astype(jnp.float32) * new_keys.astype(jnp.float32), axis=-1
    )
    row_valid = (jnp.arange(context, dtype=jnp.int32) % BLOCK).astype(jnp.float32)[
        None, :
    ] < jnp.repeat(moved_live, BLOCK, axis=1)
    pair_bits = pair_mask[0]
    partner = jnp.bitwise_xor(group_index, pair_bits)
    with_new = (jnp.arange(slot_count, dtype=jnp.int32) < slot_count - 1) | (group_index < partner)
    highest = jnp.maximum(
        jnp.max(jnp.where(row_valid[:, None, :], scores, NEGATIVE), axis=2),
        jnp.where(with_new[:, None], fresh_score, NEGATIVE),
    )
    safe_scores = jnp.where(row_valid[:, None, :], scores, highest[:, :, None])
    soft_weights = jnp.where(row_valid[:, None, :], jnp.exp(safe_scores - highest[:, :, None]), 0.0)
    fresh_weight = jnp.where(with_new[:, None], jnp.exp(fresh_score - highest), 0.0)
    weight_sum = jnp.sum(soft_weights, axis=2) + fresh_weight
    weighted = jnp.einsum(
        "jhr,jrhd->jhd",
        soft_weights.astype(jnp.bfloat16),
        value_rows,
        preferred_element_type=jnp.float32,
    )
    weighted = weighted + rounded(fresh_weight)[:, :, None] * new_values.astype(jnp.float32)
    last_high = highest[slot_count - 1 :]
    last_sum = weight_sum[slot_count - 1 :]
    last_weighted = weighted[slot_count - 1 :]
    gathered_high, gathered_sum, gathered_weighted = (
        lax.all_gather(last_high, "group", axis=0, tiled=True),
        lax.all_gather(last_sum, "group", axis=0, tiled=True),
        lax.all_gather(last_weighted, "group", axis=0, tiled=True),
    )
    picker_group = (jnp.arange(group_count, dtype=jnp.int32) == partner).astype(jnp.float32)
    other_high = jnp.sum(picker_group[:, None] * gathered_high, axis=0, keepdims=True)
    other_sum = jnp.sum(picker_group[:, None] * gathered_sum, axis=0, keepdims=True)
    other_weighted = jnp.sum(picker_group[:, None, None] * gathered_weighted, axis=0, keepdims=True)
    merged = jnp.maximum(last_high, other_high)
    own_factor = jnp.exp(last_high - merged)
    other_factor = jnp.exp(other_high - merged)
    long_sum = last_sum * own_factor + other_sum * other_factor
    long_weighted = (
        last_weighted * own_factor[:, :, None] + other_weighted * other_factor[:, :, None]
    )
    weight_sum = jnp.concatenate([weight_sum[: slot_count - 1], long_sum], axis=0)
    weighted = jnp.concatenate([weighted[: slot_count - 1], long_weighted], axis=0)
    attended = (
        (weighted / weight_sum[:, :, None]).reshape(slot_count, model_width).astype(jnp.bfloat16)
    )
    attention_out = spread_columns(attended, w_out)
    hidden = tokens.astype(jnp.float32)
    mixed = rms_normal(
        hidden + attn_rate * (rms_normal(attention_out.astype(jnp.float32)) - hidden)
    )
    mixed_low = mixed.astype(jnp.bfloat16)
    gate_factor = gate_scale * float(model_width) ** 0.5
    shard_rows = lax.all_gather(mixed_low, "shard", axis=0, tiled=True)
    up_part = jnp.dot(shard_rows, w_up, preferred_element_type=jnp.float32) * up_scale
    gate_part = jnp.dot(shard_rows, w_gate, preferred_element_type=jnp.float32) * gate_factor
    inner = (up_part * jax.nn.silu(gate_part)).astype(jnp.bfloat16)
    partial_terms = jnp.dot(inner, w_down, preferred_element_type=jnp.float32)
    mlp_out = lax.psum_scatter(
        partial_terms.astype(jnp.bfloat16), "shard", scatter_dimension=0, tiled=True
    ).astype(jnp.float32)
    new_hidden = rms_normal(mixed + mlp_rate * (rms_normal(mlp_out) - mixed)).astype(jnp.bfloat16)
    return (new_hidden, moved_cache)


def solution(mesh):
    return jax.shard_map(
        per_device,
        mesh=mesh,
        in_specs=(
            P(("group", "shard"), None),
            P(("group", "shard"), None, None),
            P(("group", "shard"), None),
            P(("group", "shard")),
            P(("group", "shard"), None),
            P(),
            P("shard", None),
            P("shard"),
            P(None, "shard"),
            P(None, "shard"),
            P(None, "shard"),
            P(None, "shard"),
            P("shard", None),
            P(),
            P(),
            P(),
            P("shard"),
            P("shard"),
        ),
        out_specs=(P(("group", "shard"), None), P(("group", "shard"), None, None)),
        check_vma=False,
    )
```

profile of v0, /device:TPU:32, one launch (start us, length us, event | category | flops | bytes accessed | tf_op | source)
XLA Modules:
  0.0 549.3 jit_solution(16223864282160331246)
XLA Ops:
  7.2 0.8 convert_element_type.140
  7.9 0.8 select_reduce_fusion.1
  8.7 0.8 fusion.64
  9.5 0.8 broadcast_select_fusion
  10.2 0.7 fusion.43
  10.9 0.1 convert_reduce_fusion
  11.1 0.2 fusion.9
  11.2 0.7 copy.91
  11.9 8.6 %all-to-all-start = ((bf16[16,1,1]{2,1,0:T(2,128)(2,1)}), bf16[16,1,1]{2,1,0:T(2,128)(2,1)S(1)}, u32[]{:S(2)}, u32[]{:S(2)}) async-start(bf16[16,1,1]{2,1,0:T(2,128)(2,1)} %copy.91), calls=%async_computation | async-start | bytes 16384 | tf_op jit(solution)/shard_map/all_to_all | solution.py:99
  20.6 0.3 reduce_window_sum.11
  20.9 23.9 %all-gather = bf16[16,2,1280]{2,1,0:T(2,128)(2,1)S(1)} all-gather(bf16[1,2,1280]{2,1,0:T(2,128)(2,1)} %bitcast.99), channel_id=1, replica_groups=mesh['group'=16,'shard'=16] {'shard'}, dimensions={0}, use_global_device_ids=true | all-gather | bytes 87040 | tf_op jit(solution)/shard_map/all_gather | solution.py:27
  44.9 1.3 convolution_convert_fusion.3
  46.2 0.6 convolution_convert_fusion.1
  46.8 0.6 all_to_all.35
  47.5 4.7 all-to-all-start.1
  52.1 6.1 %convolution_convert_fusion = bf16[16,128,2560]{2,0,1:T(8,128)(2,1)} fusion(bf16[2,128,2560]{2,1,0:T(8,128)(2,1)S(1)} %convolution_convert_fusion.1, s32[2]{0:T(128)S(1)} %fusion.43), kind=kOutput, calls=%fused_computation.2 | convolution fusion | flops 26214432 | bytes 11796488 | tf_op jit(solution)/shard_map/pj,jrc->prc/dot_general | solution.py:91
  58.2 13.7 %copy.94 = bf16[16,128,2560]{2,1,0:T(8,128)(2,1)} copy(bf16[16,128,2560]{2,0,1:T(8,128)(2,1)} %convolution_convert_fusion) | data formatting | bytes 20971520 | tf_op jit(solution)/shard_map/convert_element_type | solution.py:91
  72.0 7.4 %all-to-all-start.2 = ((bf16[16,128,2560]{2,1,0:T(8,128)(2,1)}), bf16[16,128,2560]{2,1,0:T(8,128)(2,1)}, u32[]{:S(2)}, u32[]{:S(2)}) async-start(bf16[16,128,2560]{2,1,0:T(8,128)(2,1)} %copy.94), calls=%async_computation.2 | async-start | bytes 20971520 | tf_op jit(solution)/shard_map/all_to_all | solution.py:98
  80.1 0.2 reduce.2
  80.3 0.2 convolution_bitcast_fusion
  80.6 0.1 all_to_all.38
  80.8 0.1 reshape.274
  80.8 0.1 reshape.272
  80.9 0.1 reshape.275
  81.0 0.1 multiply_reduce_fusion.2
  81.1 0.1 multiply_reduce_fusion.3
  81.2 0.2 multiply_reduce_fusion.1
  81.4 225.6 %all-to-all-done.2 = bf16[16,128,2560]{2,1,0:T(8,128)(2,1)} async-done(((bf16[16,128,2560]{2,1,0:T(8,128)(2,1)}), bf16[16,128,2560]{2,1,0:T(8,128)(2,1)}, u32[]{:S(2)}, u32[]{:S(2)}) %all-to-all-start.2) | async-done | bytes 10485792 | tf_op jit(solution)/shard_map/all_to_all | solution.py:98
  306.9 15.7 %fusion.2 = bf16[2,128,2560]{2,0,1:T(2,128)(2,1)S(1)} fusion(bf16[16,128,2560]{2,1,0:T(8,128)(2,1)} %all-to-all-done.2, s32[2]{0:T(128)S(1)} %and_select_fusion.1), kind=kOutput, calls=%fused_computation.3 | convolution fusion | flops 21626912 | bytes 11796488 | tf_op jit(solution)/shard_map/jp,prc->jrc/dot_general | solution.py:105
  322.7 1.7 fusion.65
  324.4 3.0 copy.96
  327.3 1.4 fusion.25
  328.7 0.1 select_reduce_fusion
  328.8 0.1 copy.97
  329.0 0.1 copy.98
  329.1 15.7 %all-gather.1 = f32[16,1,20]{2,1,0:T(1,128)S(1)} all-gather(f32[1,1,20]{2,1,0:T(1,128)S(1)} %slice_bitcast_fusion.1), channel_id=1, replica_groups=mesh['group'=16,'shard'=16] {'group'}, dimensions={0}, use_global_device_ids=true | all-gather | bytes 1360 | tf_op jit(solution)/shard_map/all_gather | solution.py:156
  344.8 0.1 convert_bitcast_fusion.1
  344.9 0.1 reduce_sum.137
  345.0 0.1 copy.100
  345.1 15.6 %all-gather.2 = f32[16,1,20]{2,1,0:T(1,128)S(1)} all-gather(f32[1,1,20]{2,1,0:T(1,128)S(1)} %slice_bitcast_fusion), channel_id=1, replica_groups=mesh['group'=16,'shard'=16] {'group'}, dimensions={0}, use_global_device_ids=true | all-gather | bytes 1360 | tf_op jit(solution)/shard_map/all_gather | solution.py:157
  360.7 0.1 multiply_reduce_fusion.7
  360.9 0.1 div.28
  361.0 1.9 copy.99
  362.9 1.5 fusion.23
  364.5 15.2 %all_gather.20 = f32[16,20,64]{2,1,0:T(8,128)S(1)} all-gather(f32[1,20,64]{2,1,0:T(8,128)S(1)} %slice.46), channel_id=1, replica_groups=mesh['group'=16,'shard'=16] {'group'}, dimensions={0}, use_global_device_ids=true | all-gather | bytes 87040 | tf_op jit(solution)/shard_map/all_gather | solution.py:158
  379.7 0.1 multiply_reduce_fusion
  380.1 25.8 %all-gather.3 = bf16[16,2,1280]{2,1,0:T(2,128)(2,1)} all-gather(bf16[1,2,1280]{2,1,0:T(2,128)(2,1)S(1)} %fusion.36), channel_id=1, replica_groups=mesh['group'=16,'shard'=16] {'shard'}, dimensions={0}, use_global_device_ids=true | all-gather | bytes 87040 | tf_op jit(solution)/shard_map/all_gather | solution.py:27
  405.9 0.9 reshape.284
  406.8 1.7 convolution_convert_fusion.4
  408.6 4.6 all-to-all-start.3
  413.2 7.4 %all-to-all-done.3 = bf16[16,2,80]{2,1,0:T(2,128)(2,1)S(1)} async-done(((bf16[16,2,80]{2,1,0:T(2,128)(2,1)}), bf16[16,2,80]{2,1,0:T(2,128)(2,1)S(1)}, u32[]{:S(2)}, u32[]{:S(2)}) %all-to-all-start.3) | async-done | bytes 5152 | tf_op jit(solution)/shard_map/all_to_all | solution.py:31
  420.6 0.1 reshape.276
  420.7 0.1 fusion.27
  420.9 0.2 multiply_reduce_fusion.5
  421.2 23.5 %all-gather.4 = bf16[16,2,1280]{2,1,0:T(2,128)(2,1)} all-gather(bf16[1,2,1280]{2,1,0:T(2,128)(2,1)S(1)} %fusion.35), channel_id=1, replica_groups=mesh['group'=16,'shard'=16] {'shard'}, dimensions={0}, use_global_device_ids=true | all-gather | bytes 87040 | tf_op jit(solution)/shard_map/all_gather | solution.py:183
  444.6 0.9 reshape.286
  445.6 2.1 convolution_multiply_fusion
  447.7 2.6 convolution_convert_fusion.2
  450.3 0.6 dynamic-slice
  451.5 1.2 copy.102
  452.7 87.3 %all-reduce.3.cloned.1.call-done = bf16[32,1280]{1,0:T(8,128)(2,1)} async-done(((bf16[32,1280]{1,0:T(8,128)(2,1)}), bf16[32,1280]{1,0:T(8,128)(2,1)}) %all-reduce.3.cloned.1.call-update) | async-done | bytes 81936
  540.0 0.9 fusion.30
  540.9 0.9 multiply_reduce_fusion.4
  541.8 0.7 multiply_convert_fusion.2
  (56 shorter events, 1.1 us)
Async XLA Ops:
  7.2 39.1 %copy-start = (bf16[2,128,2560]{2,1,0:T(8,128)(2,1)S(1)}, bf16[2,128,2560]{2,1,0:T(8,128)(2,1)}, u32[]{:S(2)}) copy-start(bf16[2,128,2560]{2,1,0:T(8,128)(2,1)} %param.19) | copy-start | bytes 3932164
  11.9 35.5 %all-to-all-start = ((bf16[16,1,1]{2,1,0:T(2,128)(2,1)}), bf16[16,1,1]{2,1,0:T(2,128)(2,1)S(1)}, u32[]{:S(2)}, u32[]{:S(2)}) async-start(bf16[16,1,1]{2,1,0:T(2,128)(2,1)} %copy.91), calls=%async_computation | async-start | bytes 16384 | tf_op jit(solution)/shard_map/all_to_all | solution.py:99
  47.5 24.5 %all-to-all-start.1 = ((bf16[16,2,240]{2,1,0:T(2,128)(2,1)}), bf16[16,2,240]{2,1,0:T(2,128)(2,1)S(1)}, u32[]{:S(2)}, u32[]{:S(2)}) async-start(bf16[16,2,240]{2,1,0:T(2,128)(2,1)} %all_to_all.35), calls=%async_computation.1 | async-start | bytes 32768 | tf_op jit(solution)/shard_map/all_to_all | solution.py:31
  72.0 7.4 %copy-start.4 = (f32[1280]{0:T(1024)S(1)}, f32[1280]{0:T(1024)}, u32[]{:S(2)}) copy-start(f32[1280]{0:T(1024)} %param.31) | copy-start | bytes 15364
  72.0 8.1 %copy-start.7 = (s32[1,2]{1,0:T(1,128)S(1)}, s32[1,2]{1,0:T(1,128)}, u32[]{:S(2)}) copy-start(s32[1,2]{1,0:T(1,128)} %param.24) | copy-start | bytes 28
  72.0 235.0 %all-to-all-start.2 = ((bf16[16,128,2560]{2,1,0:T(8,128)(2,1)}), bf16[16,128,2560]{2,1,0:T(8,128)(2,1)}, u32[]{:S(2)}, u32[]{:S(2)}) async-start(bf16[16,128,2560]{2,1,0:T(8,128)(2,1)} %copy.94), calls=%async_computation.2 | async-start | bytes 20971520 | tf_op jit(solution)/shard_map/all_to_all | solution.py:98
  361.0 52.2 %copy-start.6 = (f32[320]{0:T(512)S(1)}, f32[320]{0:T(512)}, u32[]{:S(2)}) copy-start(f32[320]{0:T(512)} %param.35) | copy-start | bytes 3844
  362.9 58.0 %copy-start.2 = (bf16[2,1280]{1,0:T(2,128)(2,1)S(1)}, bf16[2,1280]{1,0:T(2,128)(2,1)}, u32[]{:S(2)}) copy-start(bf16[2,1280]{1,0:T(2,128)(2,1)} %param.18) | copy-start | bytes 15364
  362.9 58.0 %copy-start.3 = (f32[1280]{0:T(1024)S(1)}, f32[1280]{0:T(1024)}, u32[]{:S(2)}) copy-start(f32[1280]{0:T(1024)} %param.32) | copy-start | bytes 15364
  364.4 83.3 %copy-start.1 = (bf16[320,1280]{1,0:T(8,128)(2,1)S(1)}, bf16[320,1280]{1,0:T(8,128)(2,1)}, u32[]{:S(2)}) copy-start(bf16[320,1280]{1,0:T(8,128)(2,1)} %param.30) | copy-start | bytes 2457604
  408.6 12.0 %all-to-all-start.3 = ((bf16[16,2,80]{2,1,0:T(2,128)(2,1)}), bf16[16,2,80]{2,1,0:T(2,128)(2,1)S(1)}, u32[]{:S(2)}, u32[]{:S(2)}) async-start(bf16[16,2,80]{2,1,0:T(2,128)(2,1)} %bitcast.27), calls=%async_computation.3 | async-start | bytes 16384 | tf_op jit(solution)/shard_map/all_to_all | solution.py:31
  413.1 126.9 %all-reduce.3.cloned.1.call-start = ((), (), s32[]{:S(2)}) async-start(), calls=%async_computation.4 | async-start | bytes 163840
  445.6 4.7 copy-start.8
  451.5 89.3 %copy-start.5 = (f32[1280]{0:T(1024)S(1)}, f32[1280]{0:T(1024)}, u32[]{:S(2)}) copy-start(f32[1280]{0:T(1024)} %param.33) | copy-start | bytes 15364
Sparse Core Ops, SparseCore 0:
  450.4 89.5 all-reduce.2
where the time goes:
time: 550 us; the launch traced here: 549 us
  waiting for transfers between devices  320 us (58%)
  blocking collectives  120 us (22%)
  matrix products  33.4 us (6%)
  local copies, waits for them, and re-layouts  26.5 us (5%)
  starting transfers between devices  25.2 us (5%)
  between operations  15.6 us (3%)
  other arithmetic  8.59 us (2%)
    all_to_all x1, waiting for transfers between devices, per_device(): lax.all_to_all(outgoing, 'group', split_axis=0, concat_axis=0, tiled=True)  226 us
    unnamed x2, waiting for transfers between devices  87.3 us
    all_gather x2, blocking collectives, spread_columns(): lax.all_gather(row_block, 'shard', axis=0, tiled=True)  49.7 us
    all_gather x1, blocking collectives, per_device(): shard_rows = lax.all_gather(mixed_low, 'shard', axis=0, tiled=True)  23.5 us
    all_gather x1, blocking collectives, per_device(): lax.all_gather(last_high, 'group', axis=0, tiled=True)  15.7 us
    dot_general x1, matrix products, per_device(): jnp.einsum('jp,prc->jrc', picker, incoming, preferred_element_type=jnp.fl...  15.7 us
    all_gather x1, blocking collectives, per_device(): lax.all_gather(last_sum, 'group', axis=0, tiled=True)  15.6 us
    all_gather x1, blocking collectives, per_device(): lax.all_gather(last_weighted, 'group', axis=0, tiled=True)  15.2 us
  transfers between devices with their start and end apart: 5, of which 3 were waited for; matrix products, arithmetic and copies ran while one was open for 5% of the time, Pallas kernels for 0%

commit v1 on v0

--- a/solution.py
+++ b/solution.py
@@ -28,7 +28,20 @@
         weight,
         preferred_element_type=jnp.float32,
     ).astype(jnp.bfloat16)
-    return lax.all_to_all(columns, "shard", split_axis=0, concat_axis=1, tiled=True)
+
+    def expand_the_pages(here_x, shard_axis):
+        z1 = jnp.concatenate(
+            lax.all_to_all(
+                jnp.stack(jnp.split(here_x, lax.axis_size(shard_axis), axis=0), axis=0),
+                axis_name=shard_axis,
+                split_axis=0,
+                concat_axis=0,
+            ),
+            axis=1,
+        )
+        return z1
+
+    return expand_the_pages(columns, "shard")
 
 
 def compact_local(kv_cache, keep_list, lengths, merge_index, merge_table):

time: 550 us -> 566 us (1.029)
  local copies, waits for them, and re-layouts: 26.5 us -> 43.3 us
    unnamed x25 -> x55, local copies, waits for them, and re-layouts: 3.71 us -> 20 us
  transfers between devices with their start and end apart: 5 -> 5, of which waited for: 3 -> 3; matrix products, arithmetic and copies ran while one was open for 5% -> 6% of each run, Pallas kernels for 0% -> 0%
where the time goes in v1:
time: 566 us; the launch traced here: 565 us
  waiting for transfers between devices  320 us (57%)
  blocking collectives  120 us (21%)
  local copies, waits for them, and re-layouts  43.3 us (8%)
  matrix products  32.7 us (6%)
  starting transfers between devices  25.3 us (4%)
  between operations  15.6 us (3%)
  other arithmetic  8.59 us (2%)
    all_to_all x1, waiting for transfers between devices, per_device(): lax.all_to_all(outgoing, 'group', split_axis=0, concat_axis=0, tiled=True)  226 us
    unnamed x2, waiting for transfers between devices  87.2 us
    all_gather x2, blocking collectives, spread_columns(): lax.all_gather(row_block, 'shard', axis=0, tiled=True)  49.7 us
    all_gather x1, blocking collectives, per_device(): shard_rows = lax.all_gather(mixed_low, 'shard', axis=0, tiled=True)  23.5 us
    unnamed x55, local copies, waits for them, and re-layouts  20 us
    all_gather x1, blocking collectives, per_device(): lax.all_gather(last_high, 'group', axis=0, tiled=True)  15.7 us
    dot_general x1, matrix products, per_device(): jnp.einsum('jp,prc->jrc', picker, incoming, preferred_element_type=jnp.fl...  15.7 us
    all_gather x1, blocking collectives, per_device(): lax.all_gather(last_sum, 'group', axis=0, tiled=True)  15.6 us
  transfers between devices with their start and end apart: 5, of which 3 were waited for; matrix products, arithmetic and copies ran while one was open for 6% of the time, Pallas kernels for 0%

profile of v1, /device:TPU:32, one launch (start us, length us, event | category | flops | bytes accessed | tf_op | source)
XLA Modules:
  0.0 565.3 jit_solution(8652213267616228055)
XLA Ops:
  7.2 0.8 convert_element_type.140
  7.9 0.8 select_reduce_fusion.1
  8.7 0.8 fusion.64
  9.5 0.8 broadcast_select_fusion
  10.2 0.7 fusion.43
  11.2 0.7 copy.90
  11.9 8.6 %all-to-all-start = ((bf16[16,1,1]{2,1,0:T(2,128)(2,1)}), bf16[16,1,1]{2,1,0:T(2,128)(2,1)S(1)}, u32[]{:S(2)}, u32[]{:S(2)}) async-start(bf16[16,1,1]{2,1,0:T(2,128)(2,1)} %copy.90), calls=%async_computation | async-start | bytes 16384 | tf_op jit(solution)/shard_map/all_to_all | solution.py:112
  20.9 23.9 %all-gather = bf16[16,2,1280]{2,1,0:T(2,128)(2,1)S(1)} all-gather(bf16[1,2,1280]{2,1,0:T(2,128)(2,1)} %bitcast.226), channel_id=1, replica_groups=mesh['group'=16,'shard'=16] {'shard'}, dimensions={0}, use_global_device_ids=true | all-gather | bytes 87040 | tf_op jit(solution)/shard_map/all_gather | solution.py:27
  44.9 1.3 convolution_convert_fusion.3
  46.2 0.6 constant_dynamic-update-slice_fusion.15
  46.8 0.6 constant_dynamic-update-slice_fusion.14
  47.4 0.6 constant_dynamic-update-slice_fusion.13
  48.0 0.6 constant_dynamic-update-slice_fusion.12
  48.5 0.6 constant_dynamic-update-slice_fusion.11
  49.1 0.6 constant_dynamic-update-slice_fusion.10
  49.7 0.6 constant_dynamic-update-slice_fusion.9
  50.2 0.6 constant_dynamic-update-slice_fusion.8
  50.8 0.6 constant_dynamic-update-slice_fusion.7
  51.4 0.6 constant_dynamic-update-slice_fusion.6
  51.9 0.6 constant_dynamic-update-slice_fusion.5
  52.5 0.6 constant_dynamic-update-slice_fusion.4
  53.1 0.6 constant_dynamic-update-slice_fusion.3
  53.6 0.6 constant_dynamic-update-slice_fusion.2
  54.2 0.6 constant_dynamic-update-slice_fusion.1
  54.8 0.5 convolution_convert_fusion.1
  55.3 0.6 constant_dynamic-update-slice_fusion
  55.9 4.7 all-to-all-start.1
  60.6 6.1 %convolution_convert_fusion = bf16[16,128,2560]{2,0,1:T(8,128)(2,1)} fusion(bf16[2,128,2560]{2,1,0:T(8,128)(2,1)S(1)} %convolution_convert_fusion.1, s32[2]{0:T(128)S(1)} %fusion.43), kind=kOutput, calls=%fused_computation.2 | convolution fusion | flops 26214432 | bytes 11796488 | tf_op jit(solution)/shard_map/pj,jrc->prc/dot_general | solution.py:104
  66.7 13.7 %copy.93 = bf16[16,128,2560]{2,1,0:T(8,128)(2,1)} copy(bf16[16,128,2560]{2,0,1:T(8,128)(2,1)} %convolution_convert_fusion) | data formatting | bytes 20971520 | tf_op jit(solution)/shard_map/convert_element_type | solution.py:104
  80.4 7.4 %all-to-all-start.2 = ((bf16[16,128,2560]{2,1,0:T(8,128)(2,1)}), bf16[16,128,2560]{2,1,0:T(8,128)(2,1)}, u32[]{:S(2)}, u32[]{:S(2)}) async-start(bf16[16,128,2560]{2,1,0:T(8,128)(2,1)} %copy.93), calls=%async_computation.2 | async-start | bytes 20971520 | tf_op jit(solution)/shard_map/all_to_all | solution.py:111
  89.8 225.6 %all-to-all-done.2 = bf16[16,128,2560]{2,1,0:T(8,128)(2,1)} async-done(((bf16[16,128,2560]{2,1,0:T(8,128)(2,1)}), bf16[16,128,2560]{2,1,0:T(8,128)(2,1)}, u32[]{:S(2)}, u32[]{:S(2)}) %all-to-all-start.2) | async-done | bytes 10485792 | tf_op jit(solution)/shard_map/all_to_all | solution.py:111
  315.4 15.7 %fusion.2 = bf16[2,128,2560]{2,0,1:T(2,128)(2,1)S(1)} fusion(bf16[16,128,2560]{2,1,0:T(8,128)(2,1)} %all-to-all-done.2, s32[2]{0:T(128)S(1)} %and_select_fusion.1), kind=kOutput, calls=%fused_computation.3 | convolution fusion | flops 21626912 | bytes 11796488 | tf_op jit(solution)/shard_map/jp,prc->jrc/dot_general | solution.py:118
  331.1 1.7 fusion.65
  332.8 3.0 copy.95
  335.8 1.4 fusion.25
  337.5 15.7 %all-gather.1 = f32[16,1,20]{2,1,0:T(1,128)S(1)} all-gather(f32[1,1,20]{2,1,0:T(1,128)S(1)} %slice_bitcast_fusion.33), channel_id=1, replica_groups=mesh['group'=16,'shard'=16] {'group'}, dimensions={0}, use_global_device_ids=true | all-gather | bytes 1360 | tf_op jit(solution)/shard_map/all_gather | solution.py:169
  353.6 15.6 %all-gather.2 = f32[16,1,20]{2,1,0:T(1,128)S(1)} all-gather(f32[1,1,20]{2,1,0:T(1,128)S(1)} %slice_bitcast_fusion.32), channel_id=1, replica_groups=mesh['group'=16,'shard'=16] {'group'}, dimensions={0}, use_global_device_ids=true | all-gather | bytes 1360 | tf_op jit(solution)/shard_map/all_gather | solution.py:170
  369.4 1.9 copy.98
  371.3 1.5 fusion.23
  372.9 15.2 %all_gather.20 = f32[16,20,64]{2,1,0:T(8,128)S(1)} all-gather(f32[1,20,64]{2,1,0:T(8,128)S(1)} %slice.46), channel_id=1, replica_groups=mesh['group'=16,'shard'=16] {'group'}, dimensions={0}, use_global_device_ids=true | all-gather | bytes 87040 | tf_op jit(solution)/shard_map/all_gather | solution.py:171
  388.5 25.7 %all-gather.3 = bf16[16,2,1280]{2,1,0:T(2,128)(2,1)} all-gather(bf16[1,2,1280]{2,1,0:T(2,128)(2,1)S(1)} %fusion.36), channel_id=1, replica_groups=mesh['group'=16,'shard'=16] {'shard'}, dimensions={0}, use_global_device_ids=true | all-gather | bytes 87040 | tf_op jit(solution)/shard_map/all_gather | solution.py:27
  414.3 0.9 reshape.288
  415.2 1.1 convolution_convert_fusion.4
  416.3 0.6 constant_dynamic-update-slice_fusion.31
  416.9 0.5 constant_dynamic-update-slice_fusion.30
  417.4 0.5 constant_dynamic-update-slice_fusion.29
  417.9 0.5 constant_dynamic-update-slice_fusion.28
  418.9 0.5 constant_dynamic-update-slice_fusion.26
  419.4 0.5 constant_dynamic-update-slice_fusion.25
  421.0 0.5 constant_dynamic-update-slice_fusion.22
  421.5 0.5 constant_dynamic-update-slice_fusion.21
  422.0 0.5 constant_dynamic-update-slice_fusion.20
  424.6 4.6 all-to-all-start.3
  429.3 7.4 %all-to-all-done.3 = bf16[16,2,80]{2,1,0:T(2,128)(2,1)S(1)} async-done(((bf16[16,2,80]{2,1,0:T(2,128)(2,1)}), bf16[16,2,80]{2,1,0:T(2,128)(2,1)S(1)}, u32[]{:S(2)}, u32[]{:S(2)}) %all-to-all-start.3) | async-done | bytes 5152 | tf_op jit(solution)/shard_map/all_to_all | solution.py:34
  437.2 23.5 %all-gather.4 = bf16[16,2,1280]{2,1,0:T(2,128)(2,1)} all-gather(bf16[1,2,1280]{2,1,0:T(2,128)(2,1)S(1)} %fusion.35), channel_id=1, replica_groups=mesh['group'=16,'shard'=16] {'shard'}, dimensions={0}, use_global_device_ids=true | all-gather | bytes 87040 | tf_op jit(solution)/shard_map/all_gather | solution.py:196
  460.7 0.9 reshape.290
  461.6 2.1 convolution_multiply_fusion
  463.8 2.6 convolution_convert_fusion.2
  466.4 0.6 dynamic-slice
  467.6 1.2 copy.101
  468.8 87.2 %all-reduce.3.cloned.1.call-done = bf16[32,1280]{1,0:T(8,128)(2,1)} async-done(((bf16[32,1280]{1,0:T(8,128)(2,1)}), bf16[32,1280]{1,0:T(8,128)(2,1)}) %all-reduce.3.cloned.1.call-update) | async-done | bytes 81936
  556.0 0.9 fusion.30
  556.9 0.9 multiply_reduce_fusion.4
  557.8 0.7 multiply_convert_fusion.2
  (87 shorter events, 7.6 us)
Async XLA Ops:
  7.2 47.6 %copy-start = (bf16[2,128,2560]{2,1,0:T(8,128)(2,1)S(1)}, bf16[2,128,2560]{2,1,0:T(8,128)(2,1)}, u32[]{:S(2)}) copy-start(bf16[2,128,2560]{2,1,0:T(8,128)(2,1)} %param.19) | copy-start | bytes 3932164
  11.9 44.0 %all-to-all-start = ((bf16[16,1,1]{2,1,0:T(2,128)(2,1)}), bf16[16,1,1]{2,1,0:T(2,128)(2,1)S(1)}, u32[]{:S(2)}, u32[]{:S(2)}) async-start(bf16[16,1,1]{2,1,0:T(2,128)(2,1)} %copy.90), calls=%async_computation | async-start | bytes 16384 | tf_op jit(solution)/shard_map/all_to_all | solution.py:112
  55.9 24.5 %all-to-all-start.1 = ((bf16[16,2,240]{2,1,0:T(2,128)(2,1)}), bf16[16,2,240]{2,1,0:T(2,128)(2,1)S(1)}, u32[]{:S(2)}, u32[]{:S(2)}) async-start(bf16[16,2,240]{2,1,0:T(2,128)(2,1)} %constant_dynamic-update-slice_fusion), calls=%async_computation.1 | async-start | bytes 32768 | tf_op jit(solution)/shard_map/all_to_all | solution.py:34
  80.4 7.4 %copy-start.4 = (f32[1280]{0:T(1024)S(1)}, f32[1280]{0:T(1024)}, u32[]{:S(2)}) copy-start(f32[1280]{0:T(1024)} %param.31) | copy-start | bytes 15364
  80.4 8.2 %copy-start.7 = (s32[1,2]{1,0:T(1,128)S(1)}, s32[1,2]{1,0:T(1,128)}, u32[]{:S(2)}) copy-start(s32[1,2]{1,0:T(1,128)} %param.24) | copy-start | bytes 28
  80.4 235.0 %all-to-all-start.2 = ((bf16[16,128,2560]{2,1,0:T(8,128)(2,1)}), bf16[16,128,2560]{2,1,0:T(8,128)(2,1)}, u32[]{:S(2)}, u32[]{:S(2)}) async-start(bf16[16,128,2560]{2,1,0:T(8,128)(2,1)} %copy.93), calls=%async_computation.2 | async-start | bytes 20971520 | tf_op jit(solution)/shard_map/all_to_all | solution.py:111
  369.4 59.8 %copy-start.6 = (f32[320]{0:T(512)S(1)}, f32[320]{0:T(512)}, u32[]{:S(2)}) copy-start(f32[320]{0:T(512)} %param.35) | copy-start | bytes 3844
  371.3 65.6 %copy-start.2 = (bf16[2,1280]{1,0:T(2,128)(2,1)S(1)}, bf16[2,1280]{1,0:T(2,128)(2,1)}, u32[]{:S(2)}) copy-start(bf16[2,1280]{1,0:T(2,128)(2,1)} %param.18) | copy-start | bytes 15364
  371.3 65.6 %copy-start.3 = (f32[1280]{0:T(1024)S(1)}, f32[1280]{0:T(1024)}, u32[]{:S(2)}) copy-start(f32[1280]{0:T(1024)} %param.32) | copy-start | bytes 15364
  372.9 90.9 %copy-start.1 = (bf16[320,1280]{1,0:T(8,128)(2,1)S(1)}, bf16[320,1280]{1,0:T(8,128)(2,1)}, u32[]{:S(2)}) copy-start(bf16[320,1280]{1,0:T(8,128)(2,1)} %param.30) | copy-start | bytes 2457604
  424.6 12.1 %all-to-all-start.3 = ((bf16[16,2,80]{2,1,0:T(2,128)(2,1)}), bf16[16,2,80]{2,1,0:T(2,128)(2,1)S(1)}, u32[]{:S(2)}, u32[]{:S(2)}) async-start(bf16[16,2,80]{2,1,0:T(2,128)(2,1)} %constant_dynamic-update-slice_fusion.16), calls=%async_computation.3 | async-start | bytes 16384 | tf_op jit(solution)/shard_map/all_to_all | solution.py:34
  429.2 126.8 %all-reduce.3.cloned.1.call-start = ((), (), s32[]{:S(2)}) async-start(), calls=%async_computation.4 | async-start | bytes 163840
  461.6 4.7 copy-start.8
  467.6 89.3 %copy-start.5 = (f32[1280]{0:T(1024)S(1)}, f32[1280]{0:T(1024)}, u32[]{:S(2)}) copy-start(f32[1280]{0:T(1024)} %param.33) | copy-start | bytes 15364
Sparse Core Ops, SparseCore 0:
  466.5 89.4 all-reduce.2
